TPU v7x, 32 devices: a whole 2x2x4 slice. The times are simulated.
32 devices in a mesh: fsdp: 8 (over z, y), ctx: 4 (over x, core).
Axes of the slice: x: 2, y: 2, z: 4, core: 2. Of those that a mesh axis runs over, the one named last changes fastest.
Arguments:
- hidden_in: bfloat16 [16, 1024, 1024], P('fsdp', 'ctx'), may hold values from -6 to 6
- segment_ids: int32 [16, 1024], P('fsdp'), may hold values from 0 to 3, never falling along the last dimension, each value on 1 to 768 neighbouring positions
- joint_weight: bfloat16 [1024, 3072], P('fsdp'), may hold values from -0.1875 to 0.1875
- joint_bias: bfloat16 [2048], P('fsdp'), may hold values from -3 to 3
- mixer_weight: bfloat16 [1024, 1024], P('fsdp'), may hold values from -1 to 1
- mixer_bias: bfloat16 [1024], P('fsdp'), may hold values from -3 to 3
- first_gain: bfloat16 [1024], P('fsdp'), may hold values from 0.5 to 1.5
- first_shift: bfloat16 [1024], P('fsdp'), may hold values from -3 to 3
- expand_weight: bfloat16 [1024, 4096], P('fsdp'), may hold values from -0.1875 to 0.1875
- expand_bias: bfloat16 [4096], P('fsdp'), may hold values from -3 to 3
- shrink_weight: bfloat16 [4096, 1024], P('fsdp'), may hold values from -0.09375 to 0.09375
- shrink_bias: bfloat16 [1024], P('fsdp'), may hold values from -3 to 3
- second_gain: bfloat16 [1024], P('fsdp'), may hold values from 0.5 to 1.5
- second_shift: bfloat16 [1024], P('fsdp'), may hold values from -3 to 3
- output_cotangent: bfloat16 [16, 1024, 1024], P('fsdp', 'ctx'), may hold values from -6 to 6
Outputs:
- layer_output: bfloat16 [16, 1024, 1024], P('fsdp', 'ctx')
- input_gradient: bfloat16 [16, 1024, 1024], P('fsdp', 'ctx')
- gradient_joint_weight: float32 [1024, 3072], P('fsdp')
- gradient_joint_bias: float32 [2048], P('fsdp')
- gradient_mixer_weight: float32 [1024, 1024], P('fsdp')
- gradient_mixer_bias: float32 [1024], P('fsdp')
- gradient_first_gain: float32 [1024], P('fsdp')
- gradient_first_shift: float32 [1024], P('fsdp')
- gradient_expand_weight: float32 [1024, 4096], P('fsdp')
- gradient_expand_bias: float32 [4096], P('fsdp')
- gradient_shrink_weight: float32 [4096, 1024], P('fsdp')
- gradient_shrink_bias: float32 [1024], P('fsdp')
- gradient_second_gain: float32 [1024], P('fsdp')
- gradient_second_shift: float32 [1024], P('fsdp')
Inputs may be any that keep to these rules, and one draw needn't show every extreme that they name: `segment_ids`: in each sequence the ids never fall, every id appears, and one document holds exactly 768 tokens.
All inputs are finite; a program needn't handle non-finite values.
Results may differ from a plain program's by a relative error of at most 0.04.
Values may be sent and summed in bfloat16 or wider, within the bound.
No kernel may reach another device: no remote copies, remote signals or barrier semaphores. Data moves between devices by JAX's collectives and lax.ppermute only.
A program may use at most 256 MiB of HBM per device.

v0:
```python
import jax
import jax.numpy as jnp
from jax import lax
from jax.sharding import PartitionSpec as P

HEAD = 64


NEG_FILL = -1e30
EPSILON = 1e-12


def as_sent(shard):

    def short(part):
        return part.astype(jnp.bfloat16) if part.dtype == jnp.float32 else part

    return jax.tree.map(short, shard)


def plain_dot(left, right):
    return jnp.dot(left, right, preferred_element_type=jnp.float32)


def left_dot(left, right):
    return lax.dot_general(
        left, right, (((0,), (0,)), ((), ())), preferred_element_type=jnp.float32
    )


def right_dot(left, right):
    return lax.dot_general(
        left, right, (((1,), (1,)), ((), ())), preferred_element_type=jnp.float32
    )


def layer_norm(values, gain, shift):
    center = values - jnp.mean(values, axis=-1, keepdims=True)
    factor = lax.rsqrt(jnp.mean(center * center, axis=-1, keepdims=True) + EPSILON)
    return center * factor * gain + shift


def gelu_exact(values):
    return jax.nn.gelu(values, approximate=False)


def block_scores(queries, keys, visible):
    scores = jnp.einsum(
        "sqhd,skhd->shqk", queries, keys, preferred_element_type=jnp.float32
    ) * HEAD ** (-0.5)
    return jnp.where(visible[:, None], scores, NEG_FILL)


def attend_block(pieces):
    queries, keys, values, visible = pieces
    scores = block_scores(queries, keys, visible)
    top = jnp.max(scores, axis=-1, keepdims=True)
    expo = jnp.exp(scores - top)
    total = jnp.sum(expo, axis=-1, keepdims=True)
    weights = (expo / total).astype(jnp.bfloat16)
    mixed = jnp.einsum("shqk,skhd->sqhd", weights, values, preferred_element_type=jnp.float32)
    return (mixed.astype(jnp.bfloat16), (top + jnp.log(total))[..., 0])


def attend_back(pieces):
    queries, keys, values, visible, summary, upstream = pieces
    scores = block_scores(queries, keys, visible)
    weights = jnp.exp(scores - summary[..., None])
    rounded = weights.astype(jnp.bfloat16)
    weight_grad = jnp.einsum(
        "sqhd,skhd->shqk", upstream, values, preferred_element_type=jnp.float32
    )
    value_grad = jnp.einsum(
        "shqk,sqhd->skhd", rounded, upstream, preferred_element_type=jnp.float32
    )
    inner = jnp.sum(weights * weight_grad, axis=-1, keepdims=True)
    score_grad = (weights * (weight_grad - inner)).astype(jnp.bfloat16)
    query_grad = jnp.einsum(
        "shqk,skhd->sqhd", score_grad, keys, preferred_element_type=jnp.float32
    ) * HEAD ** (-0.5)
    key_grad = jnp.einsum(
        "shqk,sqhd->skhd", score_grad, queries, preferred_element_type=jnp.float32
    ) * HEAD ** (-0.5)
    return (query_grad.astype(jnp.bfloat16), key_grad, value_grad)


def per_device(
    hidden_in,
    segment_ids,
    joint_weight,
    joint_bias,
    mixer_weight,
    mixer_bias,
    first_gain,
    first_shift,
    expand_weight,
    expand_bias,
    shrink_weight,
    shrink_bias,
    second_gain,
    second_shift,
    output_cotangent,
):
    seqs, local, width = hidden_in.shape
    length = segment_ids.shape[1]
    heads = width // HEAD
    rows = seqs * local
    group = min(seqs, max(1, 512 // local))
    blocks = seqs // group
    offset = lax.axis_index("ctx") * local
    query_ids = lax.dynamic_slice_in_dim(segment_ids, offset, local, 1)
    visible = (query_ids[:, :, None] == segment_ids[:, None, :]).reshape(
        blocks, group, local, length
    )
    inputs = hidden_in.reshape(rows, width)
    joint_whole, joint_offsets, mixer_whole, mixer_offsets, gain_one, shift_one = (
        lax.all_gather(joint_weight, "fsdp", axis=0, tiled=True),
        lax.all_gather(joint_bias, "fsdp", axis=0, tiled=True),
        lax.all_gather(mixer_weight, "fsdp", axis=0, tiled=True),
        lax.all_gather(mixer_bias, "fsdp", axis=0, tiled=True),
        lax.all_gather(first_gain, "fsdp", axis=0, tiled=True),
        lax.all_gather(first_shift, "fsdp", axis=0, tiled=True),
    )
    gain_one = gain_one.astype(jnp.float32)
    shift_one = shift_one.astype(jnp.float32)
    offsets = jnp.concatenate(
        [
            joint_offsets[:width].astype(jnp.float32),
            jnp.zeros((width,), jnp.float32),
            joint_offsets[width:].astype(jnp.float32),
        ]
    )
    projected = plain_dot(inputs, joint_whole) + offsets
    queries = projected[:, :width].astype(jnp.bfloat16)
    keys_mine = projected[:, width : 2 * width].astype(jnp.bfloat16).reshape(seqs, local, width)
    values_mine = projected[:, 2 * width :].astype(jnp.bfloat16).reshape(seqs, local, width)
    keys_all, values_all = (
        lax.all_gather(keys_mine, "ctx", axis=1, tiled=True),
        lax.all_gather(values_mine, "ctx", axis=1, tiled=True),
    )
    query_blocks = queries.reshape(blocks, group, local, heads, HEAD)
    key_blocks = keys_all.reshape(blocks, group, length, heads, HEAD)
    value_blocks = values_all.reshape(blocks, group, length, heads, HEAD)
    mixed, summary = lax.map(attend_block, (query_blocks, key_blocks, value_blocks, visible))
    context = mixed.reshape(rows, width)
    first_sum = (
        inputs.astype(jnp.float32)
        + plain_dot(context, mixer_whole)
        + mixer_offsets.astype(jnp.float32)
    )
    normed = layer_norm(first_sum, gain_one, shift_one)
    normed_low = normed.astype(jnp.bfloat16)
    expand_whole, expand_offsets, shrink_whole, shrink_offsets, gain_two, shift_two = (
        lax.all_gather(expand_weight, "fsdp", axis=0, tiled=True),
        lax.all_gather(expand_bias, "fsdp", axis=0, tiled=True),
        lax.all_gather(shrink_weight, "fsdp", axis=0, tiled=True),
        lax.all_gather(shrink_bias, "fsdp", axis=0, tiled=True),
        lax.all_gather(second_gain, "fsdp", axis=0, tiled=True),
        lax.all_gather(second_shift, "fsdp", axis=0, tiled=True),
    )
    gain_two = gain_two.astype(jnp.float32)
    shift_two = shift_two.astype(jnp.float32)
    lifted = plain_dot(normed_low, expand_whole) + expand_offsets.astype(jnp.float32)
    active = gelu_exact(lifted).astype(jnp.bfloat16)
    second_sum = normed + plain_dot(active, shrink_whole) + shrink_offsets.astype(jnp.float32)
    output = layer_norm(second_sum, gain_two, shift_two)
    expand_again, shrink_again = (
        lax.all_gather(expand_weight, "fsdp", axis=0, tiled=True),
        lax.all_gather(shrink_weight, "fsdp", axis=0, tiled=True),
    )
    cotangent = output_cotangent.reshape(rows, width).astype(jnp.float32)
    _, norm_two_back = jax.vjp(layer_norm, second_sum, gain_two, shift_two)
    second_grad, gain_two_grad, shift_two_grad = norm_two_back(cotangent)
    branch_low = second_grad.astype(jnp.bfloat16)
    shrink_grad = left_dot(active, branch_low)
    shrink_offsets_grad = jnp.sum(branch_low, axis=0, dtype=jnp.float32)
    active_grad = right_dot(branch_low, shrink_again)
    _, gelu_back = jax.vjp(gelu_exact, lifted)
    lifted_low = gelu_back(active_grad)[0].astype(jnp.bfloat16)
    expand_grad = left_dot(normed_low, lifted_low)
    expand_offsets_grad = jnp.sum(lifted_low, axis=0, dtype=jnp.float32)
    normed_grad = second_grad + right_dot(lifted_low, expand_again)
    expand_part = (
        lax.psum_scatter(expand_grad, "fsdp", scatter_dimension=0, tiled=True),
        lax.psum_scatter(expand_offsets_grad, "fsdp", scatter_dimension=0, tiled=True),
    )
    shrink_part = (
        lax.psum_scatter(shrink_grad, "fsdp", scatter_dimension=0, tiled=True),
        lax.psum_scatter(shrink_offsets_grad, "fsdp", scatter_dimension=0, tiled=True),
        lax.psum_scatter(gain_two_grad, "fsdp", scatter_dimension=0, tiled=True),
        lax.psum_scatter(shift_two_grad, "fsdp", scatter_dimension=0, tiled=True),
    )
    joint_again, mixer_again = (
        lax.all_gather(joint_weight, "fsdp", axis=0, tiled=True),
        lax.all_gather(mixer_weight, "fsdp", axis=0, tiled=True),
    )
    _, norm_one_back = jax.vjp(layer_norm, first_sum, gain_one, shift_one)
    first_grad, gain_one_grad, shift_one_grad = norm_one_back(normed_grad)
    branch_in = first_grad.astype(jnp.bfloat16)
    mixer_grad = left_dot(context, branch_in)
    mixer_offsets_grad = jnp.sum(branch_in, axis=0, dtype=jnp.float32)
    context_grad = right_dot(branch_in, mixer_again).astype(jnp.bfloat16)
    upstream_blocks = context_grad.reshape(blocks, group, local, heads, HEAD)
    query_grad, key_part, value_part = lax.map(
        attend_back, (query_blocks, key_blocks, value_blocks, visible, summary, upstream_blocks)
    )
    key_sum, value_sum = (
        lax.psum_scatter(
            key_part.reshape(seqs, length, width).astype(jnp.bfloat16),
            "ctx",
            scatter_dimension=1,
            tiled=True,
        ).astype(jnp.float32),
        lax.psum_scatter(
            value_part.reshape(seqs, length, width).astype(jnp.bfloat16),
            "ctx",
            scatter_dimension=1,
            tiled=True,
        ).astype(jnp.float32),
    )
    query_low = query_grad.reshape(rows, width)
    value_low = value_sum.reshape(rows, width).astype(jnp.bfloat16)
    joint_low = jnp.concatenate(
        [query_low, key_sum.reshape(rows, width).astype(jnp.bfloat16), value_low], axis=1
    )
    joint_grad = left_dot(inputs, joint_low)
    joint_offsets_grad = jnp.concatenate(
        [
            jnp.sum(query_low, axis=0, dtype=jnp.float32),
            jnp.sum(value_low, axis=0, dtype=jnp.float32),
        ]
    )
    input_grad = first_grad + right_dot(joint_low, joint_again)
    attention_part = (
        lax.psum_scatter(joint_grad, "fsdp", scatter_dimension=0, tiled=True),
        lax.psum_scatter(joint_offsets_grad, "fsdp", scatter_dimension=0, tiled=True),
        lax.psum_scatter(mixer_grad, "fsdp", scatter_dimension=0, tiled=True),
        lax.psum_scatter(mixer_offsets_grad, "fsdp", scatter_dimension=0, tiled=True),
        lax.psum_scatter(gain_one_grad, "fsdp", scatter_dimension=0, tiled=True),
        lax.psum_scatter(shift_one_grad, "fsdp", scatter_dimension=0, tiled=True),
    )
    summed = jax.tree.map(
        lambda part: part.astype(jnp.float32),
        lax.psum(as_sent(attention_part + expand_part + shrink_part), "ctx"),
    )
    return (
        output.astype(jnp.bfloat16).reshape(seqs, local, width),
        input_grad.astype(jnp.bfloat16).reshape(seqs, local, width),
        summed[0],
        summed[1],
        summed[2],
        summed[3],
        summed[4],
        summed[5],
        summed[6],
        summed[7],
        summed[8],
        summed[9],
        summed[10],
        summed[11],
    )


def solution(mesh):
    return jax.shard_map(
        per_device,
        mesh=mesh,
        in_specs=(
            P("fsdp", "ctx", None),
            P("fsdp", None),
            P("fsdp", None),
            P("fsdp"),
            P("fsdp", None),
            P("fsdp"),
            P("fsdp"),
            P("fsdp"),
            P("fsdp", None),
            P("fsdp"),
            P("fsdp", None),
            P("fsdp"),
            P("fsdp"),
            P("fsdp"),
            P("fsdp", "ctx", None),
        ),
        out_specs=(
            P("fsdp", "ctx", None),
            P("fsdp", "ctx", None),
            P("fsdp", None),
            P("fsdp"),
            P("fsdp", None),
            P("fsdp"),
            P("fsdp"),
            P("fsdp"),
            P("fsdp", None),
            P("fsdp"),
            P("fsdp", None),
            P("fsdp"),
            P("fsdp"),
            P("fsdp"),
        ),
        check_vma=False,
    )
```

profile of v0, /device:TPU:0, one launch (start us, length us, event | category | flops | bytes accessed | tf_op | source)
XLA Modules:
  0.0 1625.6 jit_solution(17009873311544838325)
XLA Ops:
  8.6 22.7 %all-gather = bf16[8,1,256]{2,1,0:T(2,128)(2,1)S(1)} all-gather(bf16[1,1,256]{2,1,0:T(2,128)(2,1)S(1)} %reshape.172), channel_id=1, replica_groups=mesh['fsdp'=8,'ctx'=4] {'fsdp'}, dimensions={0}, use_global_device_ids=true | all-gather | bytes 4608 | tf_op jit(solution)/shard_map/all_gather | solution.py:118
  31.4 80.3 %all-gather.15.cloned.1.call-done = bf16[1024,3072]{1,0:T(8,128)(2,1)} async-done(((bf16[128,3072]{1,0:T(8,128)(2,1)}), bf16[1024,3072]{1,0:T(8,128)(2,1)}) %all-gather.15.cloned.1.call-update) | async-done | bytes 6291472 | tf_op jit(solution)/shard_map/all_gather | solution.py:117
  111.6 6.5 add_convert_fusion.1
  122.6 17.7 %all-gather.1 = bf16[8,1,128]{2,1,0:T(2,128)(2,1)S(1)} all-gather(bf16[1,1,128]{2,1,0:T(2,128)(2,1)S(1)} %bitcast.128), channel_id=1, replica_groups=mesh['fsdp'=8,'ctx'=4] {'fsdp'}, dimensions={0}, use_global_device_ids=true | all-gather | bytes 2304 | tf_op jit(solution)/shard_map/all_gather | solution.py:120
  140.3 16.9 %all-gather.2 = bf16[8,1,128]{2,1,0:T(2,128)(2,1)S(1)} all-gather(bf16[1,1,128]{2,1,0:T(2,128)(2,1)S(1)} %bitcast.129), channel_id=1, replica_groups=mesh['fsdp'=8,'ctx'=4] {'fsdp'}, dimensions={0}, use_global_device_ids=true | all-gather | bytes 2304 | tf_op jit(solution)/shard_map/all_gather | solution.py:121
  157.2 17.7 %all-gather.3 = bf16[8,1,128]{2,1,0:T(2,128)(2,1)S(1)} all-gather(bf16[1,1,128]{2,1,0:T(2,128)(2,1)S(1)} %bitcast.130), channel_id=1, replica_groups=mesh['fsdp'=8,'ctx'=4] {'fsdp'}, dimensions={0}, use_global_device_ids=true | all-gather | bytes 2304 | tf_op jit(solution)/shard_map/all_gather | solution.py:122
  174.9 16.9 %all-gather.5 = bf16[8,1,128]{2,1,0:T(2,128)(2,1)S(1)} all-gather(bf16[1,1,128]{2,1,0:T(2,128)(2,1)S(1)} %bitcast.131), channel_id=1, replica_groups=mesh['fsdp'=8,'ctx'=4] {'fsdp'}, dimensions={0}, use_global_device_ids=true | all-gather | bytes 2304 | tf_op jit(solution)/shard_map/all_gather | solution.py:157
  191.8 17.8 %all-gather.6 = bf16[8,1,128]{2,1,0:T(2,128)(2,1)S(1)} all-gather(bf16[1,1,128]{2,1,0:T(2,128)(2,1)S(1)} %bitcast.132), channel_id=1, replica_groups=mesh['fsdp'=8,'ctx'=4] {'fsdp'}, dimensions={0}, use_global_device_ids=true | all-gather | bytes 2304 | tf_op jit(solution)/shard_map/all_gather | solution.py:158
  209.6 17.0 %all-gather.7 = bf16[8,1,128]{2,1,0:T(2,128)(2,1)S(1)} all-gather(bf16[1,1,128]{2,1,0:T(2,128)(2,1)S(1)} %bitcast.133), channel_id=1, replica_groups=mesh['fsdp'=8,'ctx'=4] {'fsdp'}, dimensions={0}, use_global_device_ids=true | all-gather | bytes 2304 | tf_op jit(solution)/shard_map/all_gather | solution.py:159
  226.6 26.3 %all-gather.4 = bf16[8,1,512]{2,1,0:T(2,128)(2,1)S(1)} all-gather(bf16[1,1,512]{2,1,0:T(2,128)(2,1)S(1)} %reshape.180), channel_id=1, replica_groups=mesh['fsdp'=8,'ctx'=4] {'fsdp'}, dimensions={0}, use_global_device_ids=true | all-gather | bytes 9216 | tf_op jit(solution)/shard_map/all_gather | solution.py:155
  257.5 6.7 copy.53
  264.1 16.1 fusion.35
  280.2 6.2 copy.51
  286.4 14.8 fusion
  301.2 15.1 fusion.22
  317.7 3.6 fusion.36
  321.7 44.0 %all-gather.23.cloned.1.call-done = bf16[1024,4096]{1,0:T(8,128)(2,1)} async-done(((bf16[128,4096]{1,0:T(8,128)(2,1)}), bf16[1024,4096]{1,0:T(8,128)(2,1)}) %all-gather.23.cloned.1.call-update) | async-done | bytes 8388624 | tf_op jit(solution)/shard_map/all_gather | solution.py:154
  365.7 27.9 %multiply_convert_fusion.2 = (bf16[512,4096]{1,0:T(8,128)(2,1)}, f32[512,4096]{1,0:T(8,128)}, f32[512,4096]{1,0:T(8,128)}) fusion(f32[4096]{0:T(1024)S(1)} %bitcast.115, bf16[1024,4096]{1,0:T(8,128)(2,1)} %all-gather.23.cloned.1.call-done, f32[512,1024]{1,0:T(8,128)S(1)} %get-tuple-element.153, f32[1024]{0:T(1024)S(1)} %bitcast.124, ...), kind=kOutput, calls=%fused_computation.16 | convolution fusion | flops 4436000768 | bytes 31485952 | tf_op jit(solution)/shard_map/dot_general | solution.py:22
  393.7 96.7 %all-gather.25.cloned.1.call-done = bf16[4096,1024]{1,0:T(8,128)(2,1)} async-done(((bf16[512,1024]{1,0:T(8,128)(2,1)}), bf16[4096,1024]{1,0:T(8,128)(2,1)}) %all-gather.25.cloned.1.call-update) | async-done | bytes 8388624 | tf_op jit(solution)/shard_map/all_gather | solution.py:156
  490.4 8.5 fusion.37
  503.4 14.3 convert_reduce_fusion
  517.7 9.1 multiply_reduce_fusion.1
  531.5 2.3 reshape.208
  533.8 2.8 copy.57
  536.6 15.4 fusion.12
  551.9 6.4 copy.62
  558.4 25.4 %multiply_reduce_fusion = (f32[2,16,256]{2,1,0:T(8,128)S(1)}, f32[2,16,256,1024]{3,2,1,0:T(8,128)}) fusion(f32[2,16,256,1024]{3,2,1,0:T(8,128)} %get-tuple-element.151, f32[2,16,256]{2,1,0:T(8,128)S(1)} %log_add_fusion, bf16[2,256,16,64]{1,3,2,0:T(8,128)(2,1)S(1)} %copy.57, bf16[2,1024,16,64]{1,3,2,0:T(8,128)(2,1)} %bitcast.94), kind=kOutput, calls=%fused_computation.1 | convolution fusion | flops 1098899456 | bytes 72417280 | tf_op jit(solution)/shard_map/while/body/eval_jaxpr/sqhd,skhd->shqk/dot_general | solution.py:70
  583.8 28.1 %multiply_convert_fusion = bf16[2,16,256,1024]{3,2,1,0:T(8,128)(2,1)} fusion(f32[2,16,256,1024]{3,2,1,0:T(8,128)} %get-tuple-element.159, f32[2,16,256,1024]{3,2,1,0:T(8,128)} %get-tuple-element.151, f32[2,16,256]{2,1,0:T(8,128)S(1)} %get-tuple-element.158, f32[2,16,256]{2,1,0:T(8,128)S(1)} %log_add_fusion), kind=kLoop, calls=%fused_computation | loop fusion | flops 33554432 | bytes 83951616 | tf_op jit(solution)/shard_map/while/body/eval_jaxpr/convert_element_type | solution.py:77
  611.9 10.7 multiply_convert_fusion.1
  622.6 6.3 copy.60
  629.0 4.4 fusion.38
  633.5 11.7 fusion.27
  646.5 10.4 fusion.39
  657.1 10.4 convert_reduce_fusion.5
  672.6 11.5 convolution_bitcast_fusion
  684.2 78.7 %reduce-scatter.13.cloned.1.call-done = f32[128,1024]{1,0:T(8,128)} async-done(((f32[1024,1024]{1,0:T(8,128)}), f32[128,1024]{1,0:T(8,128)}) %reduce-scatter.13.cloned.1.call-update) | async-done | bytes 524304 | tf_op jit(solution)/shard_map/reduce_scatter | solution.py:237
  764.7 281.2 %reduce-scatter.15.cloned.1.call-done = f32[128,4096]{1,0:T(8,128)} async-done(((f32[1024,4096]{1,0:T(8,128)}), f32[128,4096]{1,0:T(8,128)}) %reduce-scatter.15.cloned.1.call-update) | async-done | bytes 2097168 | tf_op jit(solution)/shard_map/reduce_scatter | solution.py:184
  1045.9 2.8 convert_element_type.260
  1048.7 279.9 %reduce-scatter.17.cloned.1.call-done = f32[512,1024]{1,0:T(8,128)} async-done(((f32[4096,1024]{1,0:T(8,128)}), f32[512,1024]{1,0:T(8,128)}) %reduce-scatter.17.cloned.1.call-update) | async-done | bytes 2097168 | tf_op jit(solution)/shard_map/reduce_scatter | solution.py:188
  1328.6 2.7 convert_element_type.265
  1331.4 207.7 %reduce-scatter.11.cloned.1.call-done = f32[128,3072]{0,1:T(8,128)} async-done(((f32[1024,3072]{0,1:T(8,128)}), f32[128,3072]{0,1:T(8,128)}) %reduce-scatter.11.cloned.1.call-update) | async-done | bytes 1572880 | tf_op jit(solution)/shard_map/reduce_scatter | solution.py:235
  1539.1 2.4 convert_element_type.245
  1545.8 35.6 %all-reduce.8 = (bf16[2048]{0:T(1024)(128)(2,1)S(1)}, bf16[1024]{0:T(1024)(128)(2,1)S(1)}, bf16[1024]{0:T(1024)(128)(2,1)S(1)}, bf16[1024]{0:T(1024)(128)(2,1)S(...) all-reduce(f32[2048]{0:T(1024)S(1)} %pad_maximum_fusion.4, ...), channel_id=5, replica_groups=mesh['fsdp'=8,'ctx'=4] {'fsdp'}, use_global_device_ids=true, to_apply=%region_17.18.clone | all-reduce | flops 12288 | bytes 73728
  1582.0 6.9 all-reduce.9
  1593.1 8.3 add_convert_fusion.2
  1601.5 8.7 all-reduce.13.cloned.1.call-done
  1612.0 2.5 copy.65
  1614.6 2.8 convert_element_type.261
  (155 shorter events, 40.1 us)
Async XLA Ops:
  7.2 104.5 %all-gather.15.cloned.1.call-start = ((), (), s32[]{:S(2)}) async-start(), calls=%async_computation.6 | async-start | bytes 7077888 | tf_op jit(solution)/shard_map/all_gather | solution.py:117
  7.9 249.5 %all-gather.19.cloned.1.call-start = ((), (), s32[]{:S(2)}) async-start(), calls=%async_computation.8 | async-start | bytes 5242880 | tf_op jit(solution)/shard_map/all_gather | solution.py:138
  118.2 4.4 copy-start.21
  118.2 4.4 copy-start.22
  118.2 22.1 %copy-start.23 = (bf16[128]{0:T(256)(128)(2,1)S(1)}, bf16[128]{0:T(256)(128)(2,1)}, u32[]{:S(2)}) copy-start(bf16[128]{0:T(256)(128)(2,1)} %param.21) | copy-start | bytes 772
  118.2 39.0 %copy-start.24 = (bf16[128]{0:T(256)(128)(2,1)S(1)}, bf16[128]{0:T(256)(128)(2,1)}, u32[]{:S(2)}) copy-start(bf16[128]{0:T(256)(128)(2,1)} %param.22) | copy-start | bytes 772
  118.2 56.7 %copy-start.25 = (bf16[128]{0:T(256)(128)(2,1)S(1)}, bf16[128]{0:T(256)(128)(2,1)}, u32[]{:S(2)}) copy-start(bf16[128]{0:T(256)(128)(2,1)} %param.26) | copy-start | bytes 772
  118.3 73.5 %copy-start.26 = (bf16[128]{0:T(256)(128)(2,1)S(1)}, bf16[128]{0:T(256)(128)(2,1)}, u32[]{:S(2)}) copy-start(bf16[128]{0:T(256)(128)(2,1)} %param.27) | copy-start | bytes 772
  118.3 91.3 %copy-start.27 = (bf16[128]{0:T(256)(128)(2,1)S(1)}, bf16[128]{0:T(256)(128)(2,1)}, u32[]{:S(2)}) copy-start(bf16[128]{0:T(256)(128)(2,1)} %param.28) | copy-start | bytes 772
  118.3 134.6 %copy-start.20 = (s32[2,1024]{1,0:T(2,128)S(1)}, s32[2,1024]{1,0:T(2,128)}, u32[]{:S(2)}) copy-start(s32[2,1024]{1,0:T(2,128)} %param.16) | copy-start | bytes 24580
  120.1 160.1 %all-gather.17.cloned.1.call-start = ((), (), s32[]{:S(2)}) async-start(), calls=%async_computation.7 | async-start | bytes 5242880 | tf_op jit(solution)/shard_map/all_gather | solution.py:139
  120.8 196.9 %all-gather.21.cloned.1.call-start = ((), (), s32[]{:S(2)}) async-start(), calls=%async_computation.9 | async-start | bytes 2359296 | tf_op jit(solution)/shard_map/all_gather | solution.py:119
  121.4 244.4 %all-gather.23.cloned.1.call-start = ((), (), s32[]{:S(2)}) async-start(), calls=%async_computation.10 | async-start | bytes 9437184 | tf_op jit(solution)/shard_map/all_gather | solution.py:154
  122.0 368.4 %all-gather.25.cloned.1.call-start = ((), (), s32[]{:S(2)}) async-start(), calls=%async_computation.11 | async-start | bytes 9437184 | tf_op jit(solution)/shard_map/all_gather | solution.py:156
  122.5 546.3 %reduce-scatter.9.cloned.1.call-start = ((), (), s32[]{:S(2)}) async-start(), calls=%async_computation.13 | async-start | bytes 5242880 | tf_op jit(solution)/shard_map/reduce_scatter | solution.py:214
  257.4 22.8 %copy-start = (bf16[2,256,16,64]{1,3,2,0:T(8,128)(2,1)}, bf16[2,256,16,64]{1,3,2,0:T(8,128)(2,1)S(1)}, u32[]{:S(2)}) copy-start(bf16[2,256,16,64]{1,3,2,0:T(8,128)(2,1)S(1)} %copy.54) | copy-start | bytes 3145732
  257.4 6.7 copy-start.8
  317.7 76.0 %copy-start.6 = (bf16[128,8,2,256]{3,1,2,0:T(8,128)(2,1)}, bf16[128,8,2,256]{3,1,2,0:T(8,128)(2,1)S(1)}, u32[]{:S(2)}) copy-start(bf16[128,8,2,256]{3,1,2,0:T(8,128)(2,1)S(1)} %copy.70) | copy-start | bytes 3145732
  490.4 8.9 copy-start.2
  503.4 14.3 copy-start.14
  517.7 9.1 copy-start.29
  526.9 3.3 copy-start.9
  527.6 1.3 copy-start.4
  529.2 1.0 copy-start.16
  558.3 112.6 %reduce-scatter.7.cloned.1.call-start = ((), (), s32[]{:S(2)}) async-start(), calls=%async_computation.12 | async-start | bytes 5242880 | tf_op jit(solution)/shard_map/reduce_scatter | solution.py:208
  583.8 28.1 %copy-start.1 = (bf16[2,256,16,64]{1,3,2,0:T(8,128)(2,1)S(1)}, bf16[2,256,16,64]{1,3,2,0:T(8,128)(2,1)}, u32[]{:S(2)}) copy-start(bf16[2,256,16,64]{1,3,2,0:T(8,128)(2,1)} %copy-done) | copy-start | bytes 3145732
  622.6 6.4 copy-start.7
  629.0 134.0 %reduce-scatter.13.cloned.1.call-start = ((), (), s32[]{:S(2)}) async-start(), calls=%async_computation.15 | async-start | bytes 4718592 | tf_op jit(solution)/shard_map/reduce_scatter | solution.py:237
  633.5 412.5 %reduce-scatter.15.cloned.1.call-start = ((), (), s32[]{:S(2)}) async-start(), calls=%async_computation.16 | async-start | bytes 18874368 | tf_op jit(solution)/shard_map/reduce_scatter | solution.py:184
  645.2 1.4 copy-start.15
  645.2 683.4 %reduce-scatter.17.cloned.1.call-start = ((), (), s32[]{:S(2)}) async-start(), calls=%async_computation.17 | async-start | bytes 18874368 | tf_op jit(solution)/shard_map/reduce_scatter | solution.py:188
  657.0 882.1 %reduce-scatter.11.cloned.1.call-start = ((), (), s32[]{:S(2)}) async-start(), calls=%async_computation.14 | async-start | bytes 14155776 | tf_op jit(solution)/shard_map/reduce_scatter | solution.py:235
  668.8 15.3 copy-start.11
  670.7 13.4 copy-start.12
  672.6 11.6 copy-start.13
  684.2 857.3 %copy-start.3 = (bf16[2,256,1024]{2,1,0:T(8,128)(2,1)S(1)}, bf16[2,256,1024]{2,1,0:T(8,128)(2,1)}, u32[]{:S(2)}) copy-start(bf16[2,256,1024]{2,1,0:T(8,128)(2,1)} %param.29) | copy-start | bytes 3145732
  684.2 926.0 %all-reduce.13.cloned.1.call-start = ((), (), s32[]{:S(2)}) async-start(), calls=%async_computation.18 | async-start | bytes 6291456 | tf_op jit(solution)/shard_map/psum | solution.py:244
  764.7 777.0 %copy-start.28 = (u32[32]{0:T(128)S(1)}, u32[32]{0:T(128)}, u32[]{:S(2)}) copy-start(u32[32]{0:T(128)} %constant.145) | copy-start | bytes 388
  764.7 781.0 %copy-start.17 = (f32[1024]{0:T(1024)S(1)}, f32[1024]{0:T(1024)}, u32[]{:S(2)}) copy-start(f32[1024]{0:T(1024)} %get-tuple-element.109) | copy-start | bytes 12292
  764.7 781.0 %copy-start.18 = (f32[1024]{0:T(1024)S(1)}, f32[1024]{0:T(1024)}, u32[]{:S(2)}) copy-start(f32[1024]{0:T(1024)} %get-tuple-element.132) | copy-start | bytes 12292
  764.7 781.0 %copy-start.19 = (f32[4096]{0:T(1024)S(1)}, f32[4096]{0:T(1024)}, u32[]{:S(2)}) copy-start(f32[4096]{0:T(1024)} %get-tuple-element.134) | copy-start | bytes 49156
  764.7 828.4 %copy-start.5 = (f32[512,1024]{1,0:T(8,128)S(1)}, f32[512,1024]{1,0:T(8,128)}, u32[]{:S(2)}) copy-start(f32[512,1024]{1,0:T(8,128)} %copy-done.4) | copy-start | bytes 6291460
  1610.1 7.2 copy-start.10
Sparse Core Ops, SparseCore 0:
  10.2 101.4 all-gather.14
  120.2 32.6 all-gather.18
  155.0 34.4 all-gather.16
  191.5 49.1 all-gather.20
  242.6 123.0 all-gather.22
  367.7 122.6 all-gather.24
  558.4 42.7 reduce-scatter.8
  629.1 41.8 reduce-scatter.6
  674.6 88.2 reduce-scatter.12
  766.6 279.3 reduce-scatter.14
  1049.7 278.8 reduce-scatter.16
  1332.1 206.9 reduce-scatter.10
  1542.2 67.8 all-reduce.12
where the time goes:
time: 1630 us
  waiting for transfers between devices  1080 us (66%)
  matrix products  211 us (13%)
  blocking collectives  195 us (12%)
  other arithmetic  71.6 us (4%)
  local copies, waits for them, and re-layouts  50 us (3%)
  between operations  16.6 us (1%)
    reduce_scatter x1, waiting for transfers between devices, per_device(): lax.psum_scatter(expand_grad, 'fsdp', scatter_dimension=0, tiled=True)  281 us
    reduce_scatter x1, waiting for transfers between devices, per_device(): lax.psum_scatter(shrink_grad, 'fsdp', scatter_dimension=0, tiled=True)  280 us
    reduce_scatter x1, waiting for transfers between devices, per_device(): lax.psum_scatter(joint_grad, 'fsdp', scatter_dimension=0, tiled=True)  208 us
    all_gather x1, waiting for transfers between devices, per_device(): lax.all_gather(shrink_weight, 'fsdp', axis=0, tiled=True)  96.7 us
    all_gather x1, waiting for transfers between devices, per_device(): lax.all_gather(joint_weight, 'fsdp', axis=0, tiled=True)  80.3 us
    reduce_scatter x1, waiting for transfers between devices, per_device(): lax.psum_scatter(mixer_grad, 'fsdp', scatter_dimension=0, tiled=True)  78.7 us
    dot_general x4, matrix products, plain_dot(): return jnp.dot(left, right, preferred_element_type=jnp.float32)  46.6 us
    all_gather x1, waiting for transfers between devices, per_device(): lax.all_gather(expand_weight, 'fsdp', axis=0, tiled=True)  44 us
  transfers between devices with their start and end apart: 13, of which 9 were waited for; matrix products, arithmetic and copies ran while one was open for 15% of the time, Pallas kernels for 0%

commit v1 on v0

v1 whole, which is shorter than its diff:
```python
import functools

import jax
import jax.numpy as jnp
from jax import lax
from jax.experimental import pallas as pl
from jax.experimental.pallas import tpu as pltpu
from jax.sharding import PartitionSpec as P

HEAD = 64
NEG_FILL = -1e30
EPSILON = 1e-12
BF = jnp.bfloat16
F32 = jnp.float32
PAD = 16


def plain_dot(left, right):
    return jnp.dot(left, right, preferred_element_type=F32)


def left_dot(left, right):
    return lax.dot_general(left, right, (((0,), (0,)), ((), ())), preferred_element_type=F32)


def right_dot(left, right):
    return lax.dot_general(left, right, (((1,), (1,)), ((), ())), preferred_element_type=F32)


def norm_stats(values):
    center = values - jnp.mean(values, axis=-1, keepdims=True)
    factor = lax.rsqrt(jnp.mean(center * center, axis=-1, keepdims=True) + EPSILON)
    return center * factor, factor


def norm_back(grad, unit, factor, gain):
    scaled = grad * gain
    return factor * (
        scaled
        - jnp.mean(scaled, axis=-1, keepdims=True)
        - unit * jnp.mean(scaled * unit, axis=-1, keepdims=True)
    )


def gelu_exact(values):
    return jax.nn.gelu(values, approximate=False)


def mask_of(key_ids, query_ids):
    return jnp.where(key_ids == query_ids, 0.0, NEG_FILL).astype(F32)


def both(mine, other, lanes):
    return jnp.concatenate([mine[:, lanes], other[:, lanes]], axis=0)


def attend_kernel(q_ref, k_ref, v_ref, ko_ref, vo_ref, kid_ref, qid_ref, o_ref, lse_ref, bias):
    @pl.when(pl.program_id(0) == 0)
    def _():
        bias[...] = mask_of(kid_ref[...], qid_ref[...])

    outs = []
    for h in range(2):
        lanes = slice(h * HEAD, (h + 1) * HEAD)
        q = q_ref[:, lanes] * jnp.asarray(HEAD ** (-0.5), BF)
        k = both(k_ref, ko_ref, lanes)
        v = both(v_ref, vo_ref, lanes)
        scores = right_dot(k, q) + bias[...]
        top = jnp.max(scores, axis=0, keepdims=True)
        expo = jnp.exp(scores - top)
        total = jnp.sum(expo, axis=0, keepdims=True)
        outs.append(left_dot(v, expo.astype(BF)) / total)
        lse_ref[0, h : h + 1, :] = top + jnp.log(total)
    o_ref[...] = jnp.concatenate(outs, axis=0).T.astype(BF)


def attend_back_kernel(
    q_ref, k_ref, v_ref, ko_ref, vo_ref, kid_ref, qid_ref, do_ref, o_ref, lse_ref,
    dq_ref, mine_ref, other_ref, bias,
):
    @pl.when(pl.program_id(0) == 0)
    def _():
        bias[...] = mask_of(kid_ref[...], qid_ref[...])

    rows = q_ref.shape[0]
    scale = HEAD ** (-0.5)
    product = (do_ref[...].astype(F32) * o_ref[...].astype(F32)).T
    dqs, dks, dvs = [], [], []
    for h in range(2):
        lanes = slice(h * HEAD, (h + 1) * HEAD)
        q = q_ref[:, lanes] * jnp.asarray(scale, BF)
        k = both(k_ref, ko_ref, lanes)
        v = both(v_ref, vo_ref, lanes)
        do = do_ref[:, lanes]
        inner = jnp.sum(product[lanes, :], axis=0, keepdims=True)
        scores = right_dot(k, q) + bias[...]
        weights = jnp.exp(scores - lse_ref[0, h : h + 1, :])
        dvs.append(plain_dot(weights.astype(BF), do))
        weight_grad = right_dot(v, do)
        score_grad = (weights * (weight_grad - inner)).astype(BF)
        dks.append(plain_dot(score_grad, q))
        dqs.append(left_dot(k, score_grad) * scale)
    dq_ref[...] = jnp.concatenate(dqs, axis=0).T.astype(BF)
    dk = jnp.concatenate(dks, axis=1).astype(BF)
    dv = jnp.concatenate(dvs, axis=1).astype(BF)
    mine_ref[0] = dk[:rows]
    mine_ref[1] = dv[:rows]
    other_ref[0] = dk[rows:]
    other_ref[1] = dv[rows:]


def attention_specs(rows, pairs):
    def column(offset):
        return pl.BlockSpec((rows, 128), lambda h, offset=offset: (0, offset + h))

    ids = [
        pl.BlockSpec((2 * rows, 1), lambda h: (0, 0)),
        pl.BlockSpec((1, rows), lambda h: (0, 0)),
    ]
    return [column(0), column(pairs), column(2 * pairs), column(0), column(pairs)] + ids, column(0)


def attend(projected, received, key_ids, query_ids):
    rows, width = projected.shape[0], projected.shape[1] // 3
    pairs = width // 128
    specs, column = attention_specs(rows, pairs)
    stats = pl.BlockSpec((1, 2, rows), lambda h: (h, 0, 0))
    return pl.pallas_call(
        attend_kernel,
        grid=(pairs,),
        in_specs=specs,
        out_specs=[column, stats],
        out_shape=[
            jax.ShapeDtypeStruct((rows, width), BF),
            jax.ShapeDtypeStruct((pairs, 2, rows), F32),
        ],
        scratch_shapes=[pltpu.VMEM((2 * rows, rows), F32)],
        name="attend",
    )(projected, projected, projected, received, received, key_ids, query_ids)


def attend_back(projected, received, key_ids, query_ids, upstream, context, stats_in):
    rows, width = projected.shape[0], projected.shape[1] // 3
    pairs = width // 128
    specs, column = attention_specs(rows, pairs)
    stats = pl.BlockSpec((1, 2, rows), lambda h: (h, 0, 0))
    double = pl.BlockSpec((2, rows, 128), lambda h: (0, 0, h))
    return pl.pallas_call(
        attend_back_kernel,
        grid=(pairs,),
        in_specs=specs + [column, column, stats],
        out_specs=[column, double, double],
        out_shape=[
            jax.ShapeDtypeStruct((rows, width), BF),
            jax.ShapeDtypeStruct((2, rows, width), BF),
            jax.ShapeDtypeStruct((2, rows, width), BF),
        ],
        scratch_shapes=[pltpu.VMEM((2 * rows, rows), F32)],
        name="attend_back",
    )(projected, projected, projected, received, received, key_ids, query_ids, upstream, context, stats_in)


class Links:
    def __init__(self, shards, parts):
        self.shards, self.parts = shards, parts
        fsdp, ctx = lax.axis_index("fsdp"), lax.axis_index("ctx")
        self.side = fsdp % 2
        self.far, self.core = ctx // 2, ctx % 2
        self.lines = [list(range(s, shards, 2)) for s in range(2)]

    def swap_side(self, item):
        return lax.ppermute(item, "fsdp", [(i, i ^ 1) for i in range(self.shards)])

    def swap_far(self, item):
        return lax.ppermute(item, "ctx", [(i, i ^ 2) for i in range(self.parts)])

    def swap_core(self, item):
        return lax.ppermute(item, "ctx", [(i, i ^ 1) for i in range(self.parts)])


def pick(item, index, axis, parts=2):
    size = item.shape[axis] // parts
    return lax.dynamic_slice_in_dim(item, index * size, size, axis)


def ordered(index, mine, other, axis):
    first = jnp.where(index == 0, mine, other)
    second = jnp.where(index == 0, other, mine)
    return jnp.concatenate([first, second], axis=axis)


def gather_rows(links, part):
    line = lax.all_gather(part, "fsdp", axis=0, axis_index_groups=links.lines)
    other = links.swap_side(line)
    first = jnp.where(links.side == 0, line, other)
    second = jnp.where(links.side == 0, other, line)
    return jnp.stack([first, second], axis=1)


def gather_weight(links, shard):
    half = gather_rows(links, pick(shard, links.core, 1))
    lines, two, rows, cols = half.shape
    half = half.reshape(lines * two * rows, cols)
    return ordered(links.core, half, links.swap_core(half), 1)


def reduce_grad(links, keep, send):
    shards, rows, cols = keep.shape
    received = links.swap_core(send)

    def side_of(item, index):
        return lax.dynamic_slice_in_dim(item.reshape(shards // 2, 2, rows, cols), index, 1, 1)[:, 0]

    def total(index):
        return (side_of(keep, index).astype(F32) + side_of(received, index).astype(F32)).astype(BF)

    crossed = links.swap_side(total(1 - links.side))
    line = (total(links.side).astype(F32) + crossed.astype(F32)).astype(BF)
    return lax.psum_scatter(
        line, "fsdp", scatter_dimension=0, tiled=True, axis_index_groups=links.lines
    )[0]


def finish_grad(links, part):
    summed = part.astype(F32) + links.swap_far(part).astype(F32)
    return summed


def per_device(
    hidden_in,
    segment_ids,
    joint_weight,
    joint_bias,
    mixer_weight,
    mixer_bias,
    first_gain,
    first_shift,
    expand_weight,
    expand_bias,
    shrink_weight,
    shrink_bias,
    second_gain,
    second_shift,
    output_cotangent,
    *,
    shards,
    parts,
):
    seqs, local, width = hidden_in.shape
    rows = seqs * local
    links = Links(shards, parts)
    far, core, side = links.far, links.core, links.side

    def share(item):
        sent = lax.dynamic_slice_in_dim(item, 1 - far, 1, 0)[0]
        kept = lax.dynamic_slice_in_dim(item, far, 1, 0)[0]
        return jnp.concatenate([kept, links.swap_far(sent)], axis=0)

    def unshare(item):
        got = links.swap_far(item[local:])
        kept = item[:local]
        return jnp.where(far == 0, jnp.stack([kept, got]), jnp.stack([got, kept]))

    small = [joint_bias, mixer_bias, first_gain, first_shift, expand_bias, shrink_bias, second_gain, second_shift]
    sizes = [item.shape[0] for item in small]
    half_cols = joint_weight.shape[1] // 2
    count = sum(sizes)
    packed = jnp.pad(jnp.concatenate(small), (0, half_cols - count)).reshape(1, half_cols)
    packed = jnp.pad(packed, ((0, PAD - 1), (0, 0)))

    inputs = share(hidden_in)
    joint_part = jnp.concatenate([pick(joint_weight, core, 1), packed], axis=0)
    joint_half = gather_rows(links, joint_part)
    lines, _, tall, _ = joint_half.shape
    short = tall - PAD
    small_whole = joint_half[:, :, short, :count].reshape(shards, count)
    joint_half = joint_half[:, :, :short].reshape(shards * short, half_cols)
    joint_whole = ordered(core, joint_half, links.swap_core(joint_half), 1)
    vectors, at = [], 0
    for size in sizes:
        vectors.append(small_whole[:, at : at + size].reshape(shards * size).astype(F32))
        at += size
    joint_offsets, mixer_offsets, gain_one, shift_one, expand_offsets, shrink_offsets, gain_two, shift_two = vectors
    offsets = jnp.concatenate([joint_offsets[:width], jnp.zeros((width,), F32), joint_offsets[width:]])

    my_ids = lax.dynamic_slice_in_dim(segment_ids, far, 1, 0)[0]

    def id_block(index):
        return lax.dynamic_slice_in_dim(my_ids, index * local, local, 0)

    own_ids = [id_block(2 * far + core), id_block(2 * (1 - far) + core)]
    partner_ids = [id_block(2 * far + 1 - core), id_block(2 * (1 - far) + 1 - core)]
    query_ids = jnp.concatenate(own_ids).reshape(1, rows)
    key_ids = jnp.concatenate(own_ids + partner_ids).reshape(2 * rows, 1)

    projected = (plain_dot(inputs, joint_whole) + offsets).astype(BF)
    received = links.swap_core(projected[:, width:])
    mixer_whole = gather_weight(links, mixer_weight)
    context, stats = attend(projected, received, key_ids, query_ids)
    expand_whole = gather_weight(links, expand_weight)
    shrink_whole = gather_weight(links, shrink_weight)
    cotangent = share(output_cotangent).astype(F32)

    first_sum = inputs.astype(F32) + plain_dot(context, mixer_whole) + mixer_offsets
    unit_one, factor_one = norm_stats(first_sum)
    normed = unit_one * gain_one + shift_one
    normed_low = normed.astype(BF)
    lifted = plain_dot(normed_low, expand_whole) + expand_offsets
    active = gelu_exact(lifted).astype(BF)
    second_sum = normed + plain_dot(active, shrink_whole) + shrink_offsets
    unit_two, factor_two = norm_stats(second_sum)
    output = unshare((unit_two * gain_two + shift_two).astype(BF))

    second_grad = norm_back(cotangent, unit_two, factor_two, gain_two)
    gain_two_grad = jnp.sum(cotangent * unit_two, axis=0)
    shift_two_grad = jnp.sum(cotangent, axis=0)
    branch_low = second_grad.astype(BF)

    def weight_grad(left, right):
        def half(index):
            piece = left_dot(left, pick(right, index, 1)).astype(BF)
            return piece.reshape(shards, piece.shape[0] // shards, piece.shape[1])

        return half(core), half(1 - core)

    shrink_part = reduce_grad(links, *weight_grad(active, branch_low))
    shrink_offsets_grad = jnp.sum(branch_low, axis=0, dtype=F32)
    _, gelu_back = jax.vjp(gelu_exact, lifted)
    lifted_low = gelu_back(right_dot(branch_low, shrink_whole))[0].astype(BF)
    expand_part = reduce_grad(links, *weight_grad(normed_low, lifted_low))
    expand_offsets_grad = jnp.sum(lifted_low, axis=0, dtype=F32)
    normed_grad = second_grad + right_dot(lifted_low, expand_whole)

    first_grad = norm_back(normed_grad, unit_one, factor_one, gain_one)
    gain_one_grad = jnp.sum(normed_grad * unit_one, axis=0)
    shift_one_grad = jnp.sum(normed_grad, axis=0)
    branch_in = first_grad.astype(BF)
    mixer_part = reduce_grad(links, *weight_grad(context, branch_in))
    mixer_offsets_grad = jnp.sum(branch_in, axis=0, dtype=F32)
    context_grad = right_dot(branch_in, mixer_whole).astype(BF)
    query_grad, kept, given = attend_back(
        projected, received, key_ids, query_ids, context_grad, context, stats
    )
    both_grads = (kept.astype(F32) + links.swap_core(given).astype(F32)).astype(BF)
    joint_low = jnp.concatenate([query_grad, both_grads[0], both_grads[1]], axis=1)
    joint_offsets_grad = jnp.concatenate(
        [jnp.sum(query_grad, axis=0, dtype=F32), jnp.sum(both_grads[1], axis=0, dtype=F32)]
    )
    small_grads = [
        joint_offsets_grad, mixer_offsets_grad, gain_one_grad, shift_one_grad,
        expand_offsets_grad, shrink_offsets_grad, gain_two_grad, shift_two_grad,
    ]
    small_rows = jnp.concatenate([item.reshape(shards, -1) for item in small_grads], axis=1).astype(BF)
    small_rows = jnp.pad(small_rows[:, None], ((0, 0), (0, PAD - 1), (0, half_cols - count)))
    joint_keep, joint_send = weight_grad(inputs, joint_low)
    joint_part = reduce_grad(
        links,
        jnp.concatenate([joint_keep, small_rows], axis=1),
        jnp.concatenate([joint_send, small_rows], axis=1),
    )
    input_grad = unshare((first_grad + right_dot(joint_low, joint_whole)).astype(BF))

    def finish(part):
        summed = (part.astype(F32) + links.swap_far(part).astype(F32)).astype(BF)
        return summed

    def widen(summed):
        return ordered(core, summed, links.swap_core(summed), 1).astype(F32)

    joint_sum = finish(joint_part)
    small_sum = joint_sum[short, :count].astype(F32)
    results, at = [], 0
    for size in sizes:
        results.append(small_sum[at : at + size])
        at += size
    joint_bias_out, mixer_bias_out, gain_one_out, shift_one_out, expand_bias_out, shrink_bias_out, gain_two_out, shift_two_out = results
    return (
        output,
        input_grad,
        widen(joint_sum[:short]),
        joint_bias_out,
        widen(finish(mixer_part)),
        mixer_bias_out,
        gain_one_out,
        shift_one_out,
        widen(finish(expand_part)),
        expand_bias_out,
        widen(finish(shrink_part)),
        shrink_bias_out,
        gain_two_out,
        shift_two_out,
    )


def solution(mesh):
    whole = P("fsdp", "ctx", None)
    matrix, vector = P("fsdp", None), P("fsdp")
    return jax.shard_map(
        functools.partial(per_device, shards=mesh.shape["fsdp"], parts=mesh.shape["ctx"]),
        mesh=mesh,
        in_specs=(
            whole, matrix, matrix, vector, matrix, vector, vector, vector,
            matrix, vector, matrix, vector, vector, vector, whole,
        ),
        out_specs=(
            whole, whole, matrix, vector, matrix, vector, vector, vector,
            matrix, vector, matrix, vector, vector, vector,
        ),
        check_vma=False,
    )
```

time: 1630 us -> 647 us (0.40)
  waiting for transfers between devices: 1080 us -> 321 us
  blocking collectives: 195 us -> 17.9 us
  matrix products: 211 us -> 104 us
  Pallas kernels: 0 us -> 45.1 us
  local copies, waits for them, and re-layouts: 50 us -> 21.4 us
  other arithmetic: 71.6 us -> 92 us
  starting transfers between devices: 0.52 us -> 20.5 us
    reduce_scatter x6 -> x4, waiting for transfers between devices: 848 us -> 2.79 us  [reduce_grad(): lax.psum_scatter(line, 'fsdp', scatter_dimension=0, tiled=True, axis_inde...]
    ppermute x0 -> x30, waiting for transfers between devices: none -> 232 us  [the longest x8 197 us: swap_side(): return lax.ppermute(item, 'fsdp', [(i, i ^ 1) for i in range(self.shards)])]
    all_gather x8 -> x1, blocking collectives: 153 us -> 17.9 us  [gather_rows(): line = lax.all_gather(part, 'fsdp', axis=0, axis_index_groups=links.lines)]
    all_gather x6 -> x3, waiting for transfers between devices: 221 us -> 86.4 us  [gather_rows(): line = lax.all_gather(part, 'fsdp', axis=0, axis_index_groups=links.lines)]
    dot_general x10 -> x4, matrix products: 140 us -> 40 us  [plain_dot(): return jnp.dot(left, right, preferred_element_type=F32)]
    pallas_call x0 -> x2, Pallas kernels: none -> 45.1 us  [the longest x1 26.3 us: attend_back(): pl.pallas_call(attend_back_kernel, grid=(pairs,), in_specs=specs + [colum...]
    unnamed x1 -> x0, blocking collectives: 35.6 us -> none
    select_n x0 -> x10, other arithmetic: none -> 22.3 us  [the longest x8 18.8 us: ordered(): first = jnp.where(index == 0, mine, other)]
  transfers between devices with their start and end apart: 13 -> 37, of which waited for: 9 -> 14; matrix products, arithmetic and copies ran while one was open for 15% -> 28% of each run, Pallas kernels for 0% -> 7%
where the time goes in v1:
time: 647 us; the launch traced here: 637 us
  waiting for transfers between devices  321 us (50%)
  matrix products  104 us (16%)
  other arithmetic  92 us (14%)
  Pallas kernels  45.1 us (7%)
  local copies, waits for them, and re-layouts  21.4 us (3%)
  starting transfers between devices  20.5 us (3%)
  blocking collectives  17.9 us (3%)
  between operations  15.6 us (2%)
    ppermute x8, waiting for transfers between devices, swap_side(): return lax.ppermute(item, 'fsdp', [(i, i ^ 1) for i in range(self.shards)])  197 us
    all_gather x3, waiting for transfers between devices, gather_rows(): line = lax.all_gather(part, 'fsdp', axis=0, axis_index_groups=links.lines)  86.4 us
    dot_general x4, matrix products, plain_dot(): return jnp.dot(left, right, preferred_element_type=F32)  40 us
    ppermute x8, waiting for transfers between devices, swap_far(): return lax.ppermute(item, 'ctx', [(i, i ^ 2) for i in range(self.parts)])  35 us
    dot_general x4, matrix products, right_dot(): lax.dot_general(left, right, (((1,), (1,)), ((), ())), preferred_element_...  33.7 us
    dot_general x8, matrix products, left_dot(): lax.dot_general(left, right, (((0,), (0,)), ((), ())), preferred_element_...  29.9 us
    pallas_call x1, Pallas kernels, attend_back(): pl.pallas_call(attend_back_kernel, grid=(pairs,), in_specs=specs + [colum...  26.3 us
    select_n x8, other arithmetic, ordered(): first = jnp.where(index == 0, mine, other)  18.8 us
  transfers between devices with their start and end apart: 37, of which 14 were waited for; matrix products, arithmetic and copies ran while one was open for 28% of the time, Pallas kernels for 7%

profile of v1, /device:TPU:0, one launch (start us, length us, event | category | flops | bytes accessed | tf_op | source)
XLA Modules:
  0.0 637.4 jit_solution(834559848477341730)
XLA Ops:
  17.9 41.2 %all-gather.8.cloned.1.call-done = bf16[576,1536]{1,0:T(8,128)(2,1)} async-done(((bf16[144,1536]{1,0:T(8,128)(2,1)}), bf16[576,1536]{1,0:T(8,128)(2,1)}) %all-gather.8.cloned.1.call-update) | async-done | bytes 1769488 | tf_op jit(solution)/shard_map/all_gather | solution.py:193
  60.6 45.2 %all-gather.10.cloned.1.call-done = bf16[512,2048]{1,0:T(8,128)(2,1)} async-done(((bf16[128,2048]{1,0:T(8,128)(2,1)}), bf16[512,2048]{1,0:T(8,128)(2,1)}) %all-gather.10.cloned.1.call-update) | async-done | bytes 2097168 | tf_op jit(solution)/shard_map/all_gather | solution.py:193
  107.3 17.9 %all-gather.1 = bf16[512,512]{1,0:T(8,128)(2,1)S(1)} all-gather(bf16[128,512]{1,0:T(8,128)(2,1)S(1)} %constant_dynamic-slice_fusion.2), channel_id=3, replica_groups={{0,8,16,24},{4,12,20,28},{1,9,17,25},{5,13,21,29},{2,10,18,26},{6,14,22..., dimensions={0}, use_global_device_ids=true | all-gather | bytes 655360 | tf_op jit(solution)/shard_map/all_gather | solution.py:193
  125.1 39.3 %collective-permute-done.4 = bf16[4,128,512]{2,1,0:T(8,128)(2,1)S(1)} collective-permute-done((bf16[4,128,512]{2,1,0:T(8,128)(2,1)S(1)}, bf16[4,128,512]{2,1,0:T(8,128)(2,1)S(1)}, u32[]{:S(2)}, u32[]{:S(2)}) %collective-permute-start.4) | collective-permute-done | bytes 524320 | tf_op jit(solution)/shard_map/ppermute | solution.py:172
  174.1 2.4 pad_maximum_fusion.7
  179.2 34.7 %collective-permute-done.8 = bf16[4,512,512]{2,1,0:T(8,128)(2,1)} collective-permute-done((bf16[4,512,512]{2,1,0:T(8,128)(2,1)}, bf16[4,512,512]{2,1,0:T(8,128)(2,1)}, u32[]{:S(2)}, u32[]{:S(2)}) %collective-permute-start.8) | collective-permute-done | bytes 2097184 | tf_op jit(solution)/shard_map/ppermute | solution.py:172
  214.0 2.5 select_bitcast_fusion.1
  216.5 2.4 pad_maximum_fusion.8
  221.2 2.9 dynamic-slice_reduce_fusion
  226.2 3.0 broadcast_select_fusion.7
  230.8 3.3 broadcast_select_fusion.5
  234.1 5.3 add_convert_fusion.1.q_ref.k_ref.v_ref
  239.9 6.4 %broadcast_select_fusion.3 = (bf16[1024,2048]{1,0:T(8,128)(2,1)}, bf16[1024,2048]{1,0:T(8,128)(2,1)}) fusion(bf16[1024,2048]{1,0:T(8,128)(2,1)} %collective-permute-done.7, pred[]{:T(512)S(6)} %eq.10, bf16[4,2,128,2048]{3,2,1,0:T(8,128)(2,1)} %pad_maximum_fusion.7), kind=kLoop, calls=%fused_computation.43 | loop fusion | flops 4194304 | bytes 16777216 | tf_op jit(solution)/shard_map/jit(_where)/select_n | solution.py:187
  246.3 5.9 broadcast_select_fusion.1
  252.2 18.7 %attend.1 = (bf16[512,1024]{1,0:T(8,128)(2,1)}, f32[8,2,512]{2,1,0:T(2,128)}) custom-call(bf16[512,3072]{1,0:T(8,128)(2,1)} %copy-done.2, bf16[512,3072]{1,0:T(8,128)(2,1)} %copy-done.2, bf16[512,3072]{1,0:T(8,128)(2,1)} %copy-done.2, bf16[512,2048]{1,0:T(8,128)(2,1)} %collective-permute-done.3.ko_ref.vo_ref, ...), custom_call_target="tpu_custom_call" | custom-call | tf_op jit(solution)/shard_map/attend/pallas_call | solution.py:128
  271.0 2.9 fusion.77
  275.0 27.2 %multiply_convert_fusion = (bf16[512,4096]{1,0:T(8,128)(2,1)S(1)}, f32[512,4096]{1,0:T(8,128)}, f32[512,4096]{1,0:T(8,128)}) fusion(f32[4096]{0:T(1024)S(1)} %bitcast.244, bf16[1024,2048]{1,0:T(8,128)(2,1)S(1)} %copy-done.8, bf16[1024,2048]{1,0:T(8,128)(2,1)S(1)} %copy-done.7, f32[512,1024]{1,0:T(8,128)S(1)} %get-tuple-element.94, ...), kind=kOutput, calls=%fused_computation.5 | convolution fusion | flops 4452777984 | bytes 31485952 | tf_op jit(solution)/shard_map/dot_general | solution.py:19
  302.2 4.7 fusion.78
  307.4 2.8 fusion.22
  310.2 3.3 fusion.72
  313.4 13.4 %fusion.79 = (bf16[4096]{0:T(1024)(128)(2,1)}, bf16[512,4096]{1,0:T(8,128)(2,1)}) fusion(f32[512,4096]{1,0:T(8,128)} %get-tuple-element.37, bf16[512,1024]{1,0:T(8,128)(2,1)} %get-tuple-element.32, bf16[4096,512]{1,0:T(8,128)(2,1)} %get-tuple-element.39, bf16[4096,512]{1,0:T(8,128)(2,1)S(1)} %copy-done.9, f32[512,4096]{1,0:T(8,128)} %get-tuple-element.95, ...), kind=kOutput, calls=%fused_computation.230 | convolution fusion | flops 4345294848 | bytes 30433280 | tf_op jit(solution)/shard_map/dot_general | solution.py:27
  326.9 6.2 convolution_convert_fusion.2
  334.5 10.5 %multiply_reduce_fusion = (bf16[1024]{0:T(1024)(128)(2,1)}, f32[512]{0:T(512)S(1)}, f32[512]{0:T(512)S(1)}, bf16[1024]{0:T(1024)(128)(2,1)}, f32[512,1024]{1,0:T(8,128)S(1)}) fusion(f32[512,1024]{1,0:T(8,128)} %copy-done.3, f32[512]{0:T(512)S(1)} %add_rsqrt_fusion.1, f32[512]{0:T(512)S(1)} %broadcast_multiply_fusion.5, f32[1024]{0:T(1024)S(1)} %get-tuple-element.79, ...), kind=kOutput, calls=%fused_computation.79 | convolution fusion | flops 4322751488 | bytes 19951616 | tf_op jit(solution)/shard_map/dot_general | solution.py:27
  345.0 2.5 fusion.74
  347.5 2.3 convolution_convert_fusion.6.do_ref
  349.8 26.3 %attend_back.1 = (bf16[512,1024]{1,0:T(8,128)(2,1)}, bf16[2,512,1024]{2,1,0:T(8,128)(2,1)}, bf16[2,512,1024]{2,1,0:T(8,128)(2,1)}) custom-call(bf16[512,3072]{1,0:T(8,128)(2,1)} %copy-done.2, bf16[512,3072]{1,0:T(8,128)(2,1)} %copy-done.2, bf16[512,3072]{1,0:T(8,128)(2,1)} %copy-done.2, bf16[512,2048]{1,0:T(8,128)(2,1)} %collective-permute-done.3.ko_ref.vo_ref, ...), custom_call_target="tpu_custom_call" | custom-call | tf_op jit(solution)/shard_map/attend_back/pallas_call | solution.py:148
  376.5 4.3 convolution_convert_fusion.3
  383.2 3.8 fusion.24
  388.6 4.5 convolution_convert_fusion
  397.8 4.4 convolution_convert_fusion.1
  402.2 44.2 %collective-permute-done.19 = bf16[4,128,512]{2,1,0:T(8,128)(2,1)S(1)} collective-permute-done((bf16[4,128,512]{2,1,0:T(8,128)(2,1)S(1)}, bf16[4,128,512]{2,1,0:T(8,128)(2,1)S(1)}, u32[]{:S(2)}, u32[]{:S(2)}) %collective-permute-start.19) | collective-permute-done | bytes 524320 | tf_op jit(solution)/shard_map/ppermute | solution.py:172
  448.8 3.2 add_convert_fusion.6
  452.8 5.7 fusion.11
  459.1 2.8 copy-done.11
  465.7 2.9 convolution_convert_fusion.4
  470.6 40.7 %collective-permute-done.27 = bf16[4,512,512]{2,1,0:T(8,128)(2,1)S(1)} collective-permute-done((bf16[4,512,512]{2,1,0:T(8,128)(2,1)S(1)}, bf16[4,512,512]{2,1,0:T(8,128)(2,1)S(1)}, u32[]{:S(2)}, u32[]{:S(2)}) %collective-permute-start.27) | collective-permute-done | bytes 2097184 | tf_op jit(solution)/shard_map/ppermute | solution.py:172
  511.3 3.8 fusion.10
  515.5 3.4 convolution_convert_fusion.5
  522.4 37.8 %collective-permute-done.15 = bf16[4,144,1536]{2,1,0:T(8,128)(2,1)S(1)} collective-permute-done((bf16[4,144,1536]{2,1,0:T(8,128)(2,1)S(1)}, bf16[4,144,1536]{2,1,0:T(8,128)(2,1)S(1)}, u32[]{:S(2)}, u32[]{:S(2)}) %collective-permute-start.15) | collective-permute-done | bytes 1769504 | tf_op jit(solution)/shard_map/ppermute | solution.py:172
  560.2 3.4 fusion.14
  565.3 7.6 %add_convert_fusion.8 = bf16[512,1024]{1,0:T(8,128)(2,1)S(1)} fusion(f32[512,1024]{1,0:T(8,128)} %get-tuple-element.35, bf16[1024,1536]{1,0:T(8,128)(2,1)} %copy-done.18, bf16[1024,1536]{1,0:T(8,128)(2,1)} %copy-done.17, bf16[512,1024]{1,0:T(8,128)(2,1)S(1)} %get-tuple-element.52, bf16[512,1024]{1,0:T(8,128)(2,1)} %copy-done.15, ...), kind=kOutput, calls=%fused_computation.80 | convolution fusion | flops 3244294144 | bytes 12582912 | tf_op jit(solution)/shard_map/dot_general | solution.py:27
  575.0 4.7 collective-permute-done.10
  579.8 2.3 maximum_select_fusion
  582.6 11.0 %collective-permute-done.20 = bf16[128,512]{1,0:T(8,128)(2,1)S(1)} collective-permute-done((bf16[128,512]{1,0:T(8,128)(2,1)}, bf16[128,512]{1,0:T(8,128)(2,1)S(1)}, u32[]{:S(2)}, u32[]{:S(2)}) %collective-permute-start.20) | collective-permute-done | bytes 131104 | tf_op jit(solution)/shard_map/ppermute | solution.py:175
  597.5 2.8 reduce-scatter.5.cloned.1.call-done
  601.8 2.6 collective-permute-done.24
  604.6 11.0 %collective-permute-done.28 = bf16[512,512]{1,0:T(8,128)(2,1)S(1)} collective-permute-done((bf16[512,512]{1,0:T(8,128)(2,1)}, bf16[512,512]{1,0:T(8,128)(2,1)S(1)}, u32[]{:S(2)}, u32[]{:S(2)}) %collective-permute-start.28) | collective-permute-done | bytes 524320 | tf_op jit(solution)/shard_map/ppermute | solution.py:175
  616.9 5.7 collective-permute-done.16
  (259 shorter events, 75.9 us)
Async XLA Ops:
  7.2 53.4 %copy-start.35 = (bf16[128,1024]{1,0:T(8,128)(2,1)S(1)}, bf16[128,1024]{1,0:T(8,128)(2,1)}, u32[]{:S(2)}) copy-start(bf16[128,1024]{1,0:T(8,128)(2,1)} %param.19) | copy-start | bytes 786436
  7.2 51.9 %all-gather.8.cloned.1.call-start = ((), (), s32[]{:S(2)}) async-start(), calls=%async_computation.8 | async-start | bytes 2211840 | tf_op jit(solution)/shard_map/all_gather | solution.py:193
  16.0 89.8 %all-gather.10.cloned.1.call-start = ((), (), s32[]{:S(2)}) async-start(), calls=%async_computation.9 | async-start | bytes 2621440 | tf_op jit(solution)/shard_map/all_gather | solution.py:193
  16.9 148.7 %all-gather.12.cloned.1.call-start = ((), (), s32[]{:S(2)}) async-start(), calls=%async_computation.10 | async-start | bytes 2621440 | tf_op jit(solution)/shard_map/all_gather | solution.py:193
  17.9 556.5 %reduce-scatter.7.cloned.1.call-start = ((), (), s32[]{:S(2)}) async-start(), calls=%async_computation.5 | async-start | bytes 655360 | tf_op jit(solution)/shard_map/reduce_scatter | solution.py:219
  59.1 107.9 %collective-permute-start.1 = (bf16[4,144,1536]{2,1,0:T(8,128)(2,1)}, bf16[4,144,1536]{2,1,0:T(8,128)(2,1)}, u32[]{:S(2)}, u32[]{:S(2)}) collective-permute-start(bf16[4,144,1536]{2,1,0:T(8,128)(2,1)} %bitcast.232), channel_id=1, source_target_pairs={{0,4},{4,0},{8,12},{12,8},{16,20},{20,16},{24,28},{28,24},{1,5},{5... | collective-permute-start | bytes 5308424 | tf_op jit(solution)/shard_map/ppermute | solution.py:172
  105.8 65.5 %collective-permute-start.6 = (bf16[4,128,2048]{2,1,0:T(8,128)(2,1)}, bf16[4,128,2048]{2,1,0:T(8,128)(2,1)}, u32[]{:S(2)}, u32[]{:S(2)}) collective-permute-start(bf16[4,128,2048]{2,1,0:T(8,128)(2,1)} %bitcast.230), channel_id=1, source_target_pairs={{0,4},{4,0},{8,12},{12,8},{16,20},{20,16},{24,28},{28,24},{1,5},{5... | collective-permute-start | bytes 6291464 | tf_op jit(solution)/shard_map/ppermute | solution.py:172
  125.1 39.3 %collective-permute-start.4 = (bf16[4,128,512]{2,1,0:T(8,128)(2,1)S(1)}, bf16[4,128,512]{2,1,0:T(8,128)(2,1)S(1)}, u32[]{:S(2)}, u32[]{:S(2)}) collective-permute-start(bf16[4,128,512]{2,1,0:T(8,128)(2,1)S(1)} %bitcast.226), channel_id=1, source_target_pairs={{0,4},{4,0},{8,12},{12,8},{16,20},{20,16},{24,28},{28,24},{1,5},{5... | collective-permute-start | bytes 1572872 | tf_op jit(solution)/shard_map/ppermute | solution.py:172
  165.6 59.1 %collective-permute-start.5 = (bf16[1024,512]{1,0:T(8,128)(2,1)}, bf16[1024,512]{1,0:T(8,128)(2,1)}, u32[]{:S(2)}, u32[]{:S(2)}) collective-permute-start(bf16[1024,512]{1,0:T(8,128)(2,1)} %bitcast.17), channel_id=1, source_target_pairs={{0,1},{1,0},{2,3},{3,2},{4,5},{5,4},{6,7},{7,6},{8,9},{9,8},{10,11... | collective-permute-start | bytes 3145736 | tf_op jit(solution)/shard_map/ppermute | solution.py:178
  165.6 48.4 %collective-permute-start.8 = (bf16[4,512,512]{2,1,0:T(8,128)(2,1)}, bf16[4,512,512]{2,1,0:T(8,128)(2,1)}, u32[]{:S(2)}, u32[]{:S(2)}) collective-permute-start(bf16[4,512,512]{2,1,0:T(8,128)(2,1)} %bitcast.228), channel_id=1, source_target_pairs={{0,4},{4,0},{8,12},{12,8},{16,20},{20,16},{24,28},{28,24},{1,5},{5... | collective-permute-start | bytes 6291464 | tf_op jit(solution)/shard_map/ppermute | solution.py:172
  171.1 59.7 %collective-permute-start.2 = (bf16[1024,1536]{1,0:T(8,128)(2,1)}, bf16[1024,1536]{1,0:T(8,128)(2,1)}, u32[]{:S(2)}, u32[]{:S(2)}) collective-permute-start(bf16[1024,1536]{1,0:T(8,128)(2,1)} %bitcast.6), channel_id=1, source_target_pairs={{0,1},{1,0},{2,3},{3,2},{4,5},{5,4},{6,7},{7,6},{8,9},{9,8},{10,11... | collective-permute-start | bytes 9437192 | tf_op jit(solution)/shard_map/ppermute | solution.py:178
  176.5 63.4 %collective-permute-start.7 = (bf16[1024,2048]{1,0:T(8,128)(2,1)}, bf16[1024,2048]{1,0:T(8,128)(2,1)}, u32[]{:S(2)}, u32[]{:S(2)}) collective-permute-start(bf16[1024,2048]{1,0:T(8,128)(2,1)} %bitcast.25), channel_id=1, source_target_pairs={{0,1},{1,0},{2,3},{3,2},{4,5},{5,4},{6,7},{7,6},{8,9},{9,8},{10,11... | collective-permute-start | bytes 12582920 | tf_op jit(solution)/shard_map/ppermute | solution.py:178
  177.8 56.4 %collective-permute-start = (bf16[256,1024]{1,0:T(8,128)(2,1)}, bf16[256,1024]{1,0:T(8,128)(2,1)}, u32[]{:S(2)}, u32[]{:S(2)}) collective-permute-start(bf16[256,1024]{1,0:T(8,128)(2,1)} %get-tuple-element.70), channel_id=1, source_target_pairs={{0,2},{1,3},{2,0},{3,1},{4,6},{5,7},{6,4},{7,5},{8,10},{9,11},{10,... | collective-permute-start | bytes 1572872 | tf_op jit(solution)/shard_map/ppermute | solution.py:175
  218.9 27.4 %collective-permute-start.9 = (bf16[4096,512]{1,0:T(8,128)(2,1)}, bf16[4096,512]{1,0:T(8,128)(2,1)}, u32[]{:S(2)}, u32[]{:S(2)}) collective-permute-start(bf16[4096,512]{1,0:T(8,128)(2,1)} %bitcast.30), channel_id=1, source_target_pairs={{0,1},{1,0},{2,3},{3,2},{4,5},{5,4},{6,7},{7,6},{8,9},{9,8},{10,11... | collective-permute-start | bytes 12582920 | tf_op jit(solution)/shard_map/ppermute | solution.py:178
  224.7 82.7 %collective-permute-start.11 = (bf16[256,1024]{1,0:T(8,128)(2,1)}, bf16[256,1024]{1,0:T(8,128)(2,1)}, u32[]{:S(2)}, u32[]{:S(2)}) collective-permute-start(bf16[256,1024]{1,0:T(8,128)(2,1)} %get-tuple-element.61), channel_id=1, source_target_pairs={{0,2},{1,3},{2,0},{3,1},{4,6},{5,7},{6,4},{7,5},{8,10},{9,11},{10,... | collective-permute-start | bytes 1572872 | tf_op jit(solution)/shard_map/ppermute | solution.py:175
  230.8 96.1 %copy-start.43 = (f32[1024]{0:T(1024)}, f32[1024]{0:T(1024)S(1)}, u32[]{:S(2)}) copy-start(f32[1024]{0:T(1024)S(1)} %get-tuple-element.78) | copy-start | bytes 12292
  239.6 12.6 %collective-permute-start.3 = (bf16[512,2048]{1,0:T(8,128)(2,1)S(1)}, bf16[512,2048]{1,0:T(8,128)(2,1)}, u32[]{:S(2)}, u32[]{:S(2)}) collective-permute-start(bf16[512,2048]{1,0:T(8,128)(2,1)S(1)} %slice.162), channel_id=1, source_target_pairs={{0,1},{1,0},{2,3},{3,2},{4,5},{5,4},{6,7},{7,6},{8,9},{9,8},{10,11... | collective-permute-start | bytes 6291464 | tf_op jit(solution)/shard_map/ppermute | solution.py:178
  273.9 53.0 %copy-start.3 = (f32[512,1024]{1,0:T(8,128)}, f32[512,1024]{1,0:T(8,128)S(1)}, u32[]{:S(2)}) copy-start(f32[512,1024]{1,0:T(8,128)S(1)} %get-tuple-element.94) | copy-start | bytes 6291460
  274.2 70.7 %copy-start.38 = (f32[512]{0:T(512)}, f32[512]{0:T(512)S(1)}, u32[]{:S(2)}) copy-start(f32[512]{0:T(512)S(1)} %add_rsqrt_fusion.1) | copy-start | bytes 6148
  275.0 27.2 %copy-start.9 = (bf16[4096,512]{1,0:T(8,128)(2,1)S(1)}, bf16[4096,512]{1,0:T(8,128)(2,1)}, u32[]{:S(2)}) copy-start(bf16[4096,512]{1,0:T(8,128)(2,1)} %get-tuple-element.38) | copy-start | bytes 12582916
  275.0 27.2 %copy-start.10 = (bf16[4096,512]{1,0:T(8,128)(2,1)S(1)}, bf16[4096,512]{1,0:T(8,128)(2,1)}, u32[]{:S(2)}) copy-start(bf16[4096,512]{1,0:T(8,128)(2,1)} %get-tuple-element.39) | copy-start | bytes 12582916
  333.1 50.2 %collective-permute-start.22 = (bf16[8,128,2048]{2,1,0:T(8,128)(2,1)}, bf16[8,128,2048]{2,1,0:T(8,128)(2,1)}, u32[]{:S(2)}, u32[]{:S(2)}) collective-permute-start(bf16[8,128,2048]{2,1,0:T(8,128)(2,1)} %bitcast.68), channel_id=1, source_target_pairs={{0,1},{1,0},{2,3},{3,2},{4,5},{5,4},{6,7},{7,6},{8,9},{9,8},{10,11... | collective-permute-start | bytes 12582920 | tf_op jit(solution)/shard_map/ppermute | solution.py:178
  349.8 26.7 %copy-start.5 = (f32[512,1024]{1,0:T(8,128)S(1)}, f32[512,1024]{1,0:T(8,128)}, u32[]{:S(2)}) copy-start(f32[512,1024]{1,0:T(8,128)} %copy-done.3) | copy-start | bytes 6291460
  349.8 26.7 %copy-start.39 = (f32[512]{0:T(512)S(1)}, f32[512]{0:T(512)}, u32[]{:S(2)}) copy-start(f32[512]{0:T(512)} %copy-done.38) | copy-start | bytes 6148
  349.8 26.7 %copy-start.44 = (f32[1024]{0:T(1024)S(1)}, f32[1024]{0:T(1024)}, u32[]{:S(2)}) copy-start(f32[1024]{0:T(1024)} %copy-done.43) | copy-start | bytes 12292
  376.1 72.7 %collective-permute-start.12 = (bf16[2,512,1024]{2,1,0:T(8,128)(2,1)}, bf16[2,512,1024]{2,1,0:T(8,128)(2,1)}, u32[]{:S(2)}, u32[]{:S(2)}) collective-permute-start(bf16[2,512,1024]{2,1,0:T(8,128)(2,1)} %get-tuple-element.23), channel_id=1, source_target_pairs={{0,1},{1,0},{2,3},{3,2},{4,5},{5,4},{6,7},{7,6},{8,9},{9,8},{10,11... | collective-permute-start | bytes 6291464 | tf_op jit(solution)/shard_map/ppermute | solution.py:178
  383.0 12.9 %collective-permute-start.18 = (bf16[8,128,512]{2,1,0:T(8,128)(2,1)}, bf16[8,128,512]{2,1,0:T(8,128)(2,1)}, u32[]{:S(2)}, u32[]{:S(2)}) collective-permute-start(bf16[8,128,512]{2,1,0:T(8,128)(2,1)} %bitcast.59), channel_id=1, source_target_pairs={{0,1},{1,0},{2,3},{3,2},{4,5},{5,4},{6,7},{7,6},{8,9},{9,8},{10,11... | collective-permute-start | bytes 3145736 | tf_op jit(solution)/shard_map/ppermute | solution.py:178
  387.1 65.7 %collective-permute-start.23 = (bf16[4,128,2048]{2,1,0:T(8,128)(2,1)}, bf16[4,128,2048]{2,1,0:T(8,128)(2,1)}, u32[]{:S(2)}, u32[]{:S(2)}) collective-permute-start(bf16[4,128,2048]{2,1,0:T(8,128)(2,1)} %fusion.24), channel_id=1, source_target_pairs={{0,4},{4,0},{8,12},{12,8},{16,20},{20,16},{24,28},{28,24},{1,5},{5... | collective-permute-start | bytes 6291464 | tf_op jit(solution)/shard_map/ppermute | solution.py:172
  393.9 65.2 %collective-permute-start.26 = (bf16[8,512,512]{2,1,0:T(8,128)(2,1)}, bf16[8,512,512]{2,1,0:T(8,128)(2,1)}, u32[]{:S(2)}, u32[]{:S(2)}) collective-permute-start(bf16[8,512,512]{2,1,0:T(8,128)(2,1)} %bitcast.256), channel_id=1, source_target_pairs={{0,1},{1,0},{2,3},{3,2},{4,5},{5,4},{6,7},{7,6},{8,9},{9,8},{10,11... | collective-permute-start | bytes 12582920 | tf_op jit(solution)/shard_map/ppermute | solution.py:178
  397.2 49.3 %collective-permute-start.19 = (bf16[4,128,512]{2,1,0:T(8,128)(2,1)S(1)}, bf16[4,128,512]{2,1,0:T(8,128)(2,1)S(1)}, u32[]{:S(2)}, u32[]{:S(2)}) collective-permute-start(bf16[4,128,512]{2,1,0:T(8,128)(2,1)S(1)} %fusion.42), channel_id=1, source_target_pairs={{0,4},{4,0},{8,12},{12,8},{16,20},{20,16},{24,28},{28,24},{1,5},{5... | collective-permute-start | bytes 1572872 | tf_op jit(solution)/shard_map/ppermute | solution.py:172
  448.5 133.6 %reduce-scatter.9.cloned.1.call-start = ((), (), s32[]{:S(2)}) async-start(), calls=%async_computation.6 | async-start | bytes 2621440 | tf_op jit(solution)/shard_map/reduce_scatter | solution.py:219
  458.5 137.6 %reduce-scatter.11.cloned.1.call-start = ((), (), s32[]{:S(2)}) async-start(), calls=%async_computation.7 | async-start | bytes 2621440 | tf_op jit(solution)/shard_map/reduce_scatter | solution.py:219
  464.1 47.1 %collective-permute-start.27 = (bf16[4,512,512]{2,1,0:T(8,128)(2,1)S(1)}, bf16[4,512,512]{2,1,0:T(8,128)(2,1)S(1)}, u32[]{:S(2)}, u32[]{:S(2)}) collective-permute-start(bf16[4,512,512]{2,1,0:T(8,128)(2,1)S(1)} %fusion.26), channel_id=1, source_target_pairs={{0,4},{4,0},{8,12},{12,8},{16,20},{20,16},{24,28},{28,24},{1,5},{5... | collective-permute-start | bytes 6291464 | tf_op jit(solution)/shard_map/ppermute | solution.py:172
  470.6 48.3 %collective-permute-start.14 = (bf16[8,144,1536]{2,1,0:T(8,128)(2,1)}, bf16[8,144,1536]{2,1,0:T(8,128)(2,1)}, u32[]{:S(2)}, u32[]{:S(2)}) collective-permute-start(bf16[8,144,1536]{2,1,0:T(8,128)(2,1)} %pad_maximum_fusion.11), channel_id=1, source_target_pairs={{0,1},{1,0},{2,3},{3,2},{4,5},{5,4},{6,7},{7,6},{8,9},{9,8},{10,11... | collective-permute-start | bytes 10616840 | tf_op jit(solution)/shard_map/ppermute | solution.py:178
  515.1 85.2 %reduce-scatter.5.cloned.1.call-start = ((), (), s32[]{:S(2)}) async-start(), calls=%async_computation.4 | async-start | bytes 2211840 | tf_op jit(solution)/shard_map/reduce_scatter | solution.py:219
  520.9 42.7 %copy-start.13 = (bf16[512,1024]{1,0:T(8,128)(2,1)S(1)}, bf16[512,1024]{1,0:T(8,128)(2,1)}, u32[]{:S(2)}) copy-start(bf16[512,1024]{1,0:T(8,128)(2,1)} %get-tuple-element.50) | copy-start | bytes 3145732
  520.9 39.3 %collective-permute-start.15 = (bf16[4,144,1536]{2,1,0:T(8,128)(2,1)S(1)}, bf16[4,144,1536]{2,1,0:T(8,128)(2,1)S(1)}, u32[]{:S(2)}, u32[]{:S(2)}) collective-permute-start(bf16[4,144,1536]{2,1,0:T(8,128)(2,1)S(1)} %fusion.34), channel_id=1, source_target_pairs={{0,4},{4,0},{8,12},{12,8},{16,20},{20,16},{24,28},{28,24},{1,5},{5... | collective-permute-start | bytes 5308424 | tf_op jit(solution)/shard_map/ppermute | solution.py:172
  564.6 15.1 %collective-permute-start.10 = (bf16[256,1024]{1,0:T(8,128)(2,1)}, bf16[256,1024]{1,0:T(8,128)(2,1)}, u32[]{:S(2)}, u32[]{:S(2)}) collective-permute-start(bf16[256,1024]{1,0:T(8,128)(2,1)} %get-tuple-element.66), channel_id=1, source_target_pairs={{0,2},{1,3},{2,0},{3,1},{4,6},{5,7},{6,4},{7,5},{8,10},{9,11},{10,... | collective-permute-start | bytes 1572872 | tf_op jit(solution)/shard_map/ppermute | solution.py:175
  573.0 21.8 %collective-permute-start.13 = (bf16[256,1024]{1,0:T(8,128)(2,1)S(1)}, bf16[256,1024]{1,0:T(8,128)(2,1)S(1)}, u32[]{:S(2)}, u32[]{:S(2)}) collective-permute-start(bf16[256,1024]{1,0:T(8,128)(2,1)S(1)} %get-tuple-element.64), channel_id=1, source_target_pairs={{0,2},{1,3},{2,0},{3,1},{4,6},{5,7},{6,4},{7,5},{8,10},{9,11},{10,... | collective-permute-start | bytes 1572872 | tf_op jit(solution)/shard_map/ppermute | solution.py:175
  574.4 19.3 %collective-permute-start.20 = (bf16[128,512]{1,0:T(8,128)(2,1)}, bf16[128,512]{1,0:T(8,128)(2,1)S(1)}, u32[]{:S(2)}, u32[]{:S(2)}) collective-permute-start(bf16[128,512]{1,0:T(8,128)(2,1)} %bitcast.240), channel_id=1, source_target_pairs={{0,2},{1,3},{2,0},{3,1},{4,6},{5,7},{6,4},{7,5},{8,10},{9,11},{10,... | collective-permute-start | bytes 393224 | tf_op jit(solution)/shard_map/ppermute | solution.py:175
  582.1 22.3 %copy-start.30 = (bf16[1,128,2048]{2,1,0:T(8,128)(2,1)S(1)}, bf16[1,128,2048]{2,1,0:T(8,128)(2,1)}, u32[]{:S(2)}) copy-start(bf16[1,128,2048]{2,1,0:T(8,128)(2,1)} %reduce-scatter.9.cloned.1.call-done) | copy-start | bytes 1572868
  582.1 22.3 %collective-permute-start.24 = (bf16[128,2048]{1,0:T(8,128)(2,1)}, bf16[128,2048]{1,0:T(8,128)(2,1)S(1)}, u32[]{:S(2)}, u32[]{:S(2)}) collective-permute-start(bf16[128,2048]{1,0:T(8,128)(2,1)} %bitcast.236), channel_id=1, source_target_pairs={{0,2},{1,3},{2,0},{3,1},{4,6},{5,7},{6,4},{7,5},{8,10},{9,11},{10,... | collective-permute-start | bytes 1572872 | tf_op jit(solution)/shard_map/ppermute | solution.py:175
  594.6 1.4 collective-permute-start.21
  596.1 19.5 %collective-permute-start.28 = (bf16[512,512]{1,0:T(8,128)(2,1)}, bf16[512,512]{1,0:T(8,128)(2,1)S(1)}, u32[]{:S(2)}, u32[]{:S(2)}) collective-permute-start(bf16[512,512]{1,0:T(8,128)(2,1)} %bitcast.237), channel_id=1, source_target_pairs={{0,2},{1,3},{2,0},{3,1},{4,6},{5,7},{6,4},{7,5},{8,10},{9,11},{10,... | collective-permute-start | bytes 1572872 | tf_op jit(solution)/shard_map/ppermute | solution.py:175
  600.3 22.2 %collective-permute-start.16 = (bf16[144,1536]{1,0:T(8,128)(2,1)}, bf16[144,1536]{1,0:T(8,128)(2,1)S(1)}, u32[]{:S(2)}, u32[]{:S(2)}) collective-permute-start(bf16[144,1536]{1,0:T(8,128)(2,1)} %bitcast.239), channel_id=1, source_target_pairs={{0,2},{1,3},{2,0},{3,1},{4,6},{5,7},{6,4},{7,5},{8,10},{9,11},{10,... | collective-permute-start | bytes 1327112 | tf_op jit(solution)/shard_map/ppermute | solution.py:175
  604.5 22.5 %collective-permute-start.25 = (bf16[128,2048]{1,0:T(8,128)(2,1)S(1)}, bf16[128,2048]{1,0:T(8,128)(2,1)S(1)}, u32[]{:S(2)}, u32[]{:S(2)}) collective-permute-start(bf16[128,2048]{1,0:T(8,128)(2,1)S(1)} %add_convert_fusion.11), channel_id=1, source_target_pairs={{0,1},{1,0},{2,3},{3,2},{4,5},{5,4},{6,7},{7,6},{8,9},{9,8},{10,11... | collective-permute-start | bytes 1572872 | tf_op jit(solution)/shard_map/ppermute | solution.py:178
  616.8 8.6 %collective-permute-start.29 = (bf16[512,512]{1,0:T(8,128)(2,1)S(1)}, bf16[512,512]{1,0:T(8,128)(2,1)S(1)}, u32[]{:S(2)}, u32[]{:S(2)}) collective-permute-start(bf16[512,512]{1,0:T(8,128)(2,1)S(1)} %add_convert_fusion.10), channel_id=1, source_target_pairs={{0,1},{1,0},{2,3},{3,2},{4,5},{5,4},{6,7},{7,6},{8,9},{9,8},{10,11... | collective-permute-start | bytes 1572872 | tf_op jit(solution)/shard_map/ppermute | solution.py:178
  625.4 3.3 collective-permute-start.17
  (40 other events, 250.2 us)
Sparse Core Ops, SparseCore 0:
  16.1 42.9 all-gather.7
  61.3 44.4 all-gather.9
  107.9 46.7 all-gather.11
  448.6 19.9 reduce-scatter.6
  471.3 41.8 reduce-scatter.8
  515.3 42.8 reduce-scatter.10
  563.7 36.5 reduce-scatter.4
